TPU v7x, 32 devices: a whole 2x2x4 slice. The times are simulated.
32 devices in a mesh: tm: 8 (over z, y), head: 4 (over x, core).
Axes of the slice: x: 2, y: 2, z: 4, core: 2. Of those that a mesh axis runs over, the one named last changes fastest.
Arguments:
- queries: bfloat16 [6144, 1536], P('tm', 'head'), may hold values from -6 to 6
- key_rows: bfloat16 [6144, 1536], P('tm', 'head'), may hold values from -6 to 6
- value_rows: bfloat16 [6144, 1536], P('tm', 'head'), may hold values from -6 to 6
- grad_out: bfloat16 [6144, 3072], P('tm', 'head'), may hold values from -192 to 192
- w_out: bfloat16 [1536, 3072], P('head', 'tm'), may hold values from -0.109375 to 0.109375
Outputs:
- grad_queries: bfloat16 [6144, 1536], P('tm', 'head')
- grad_keys: bfloat16 [6144, 1536], P('tm', 'head')
- grad_values: bfloat16 [6144, 1536], P('tm', 'head')
All inputs are finite; a program needn't handle non-finite values.
Results may differ from a plain program's by a relative error of at most 0.0081.
Values may be sent and summed in bfloat16 or wider, within the bound.
No kernel may reach another device: no remote copies, remote signals or barrier semaphores. Data moves between devices by JAX's collectives and lax.ppermute only.
A program may use at most 128 MiB of HBM per device.

v0:
```python
import math
import jax
import jax.numpy as jnp
from jax import lax
from jax.sharding import PartitionSpec as P

HD = 128
TILE_T = 6
TILE_H = 8
TILE_W = 8
VT = 8


def passed_along(block, axis, distance):
    devices = range(lax.axis_size(axis))
    route = [(i - distance, i) for i in devices if i - distance in devices]
    return lax.ppermute(block, axis, route)


def tile_range(index, count):
    return (max(index - 1, 0), min(index + 1, count - 1))


def local(queries, key_rows, value_rows, grad_out, w_out):
    token_count, local_width = queries.shape
    head_count = local_width // HD
    tile_size = TILE_T * TILE_H * TILE_W
    tile_count = token_count // tile_size
    inverse_root = 1.0 / math.sqrt(HD)
    video_place = lax.axis_index("tm") % VT
    flags = (video_place > 0, video_place >= 0, video_place < VT - 1)
    full_grad = lax.all_gather(grad_out, "head", axis=1, tiled=True)
    attn_sum = jnp.einsum(
        "td,hd->th",
        full_grad,
        lax.all_gather(w_out, "tm", axis=1, tiled=True),
        preferred_element_type=jnp.float32,
    )
    attn_grad = attn_sum.astype(jnp.bfloat16)
    before_keys, before_values = passed_along((key_rows, value_rows), "tm", 1)
    after_keys, after_values = passed_along((key_rows, value_rows), "tm", -1)
    slab_keys = (before_keys, key_rows, after_keys)
    slab_values = (before_values, value_rows, after_values)
    zero_tile = jnp.zeros((tile_size, local_width), jnp.float32)
    key_sums = [[zero_tile] * tile_count for other in range(3)]
    value_sums = [[zero_tile] * tile_count for other in range(3)]
    query_grads = []
    for tile_index in range(tile_count):
        lower, upper = tile_range(tile_index, tile_count)
        width_rows = (upper - lower + 1) * tile_size
        key_block = jnp.concatenate([part for part in slab_keys], 0)
        key_block = key_block.reshape(3 * width_rows, head_count, HD)
        value_block = jnp.concatenate([part for part in slab_values], 0)
        value_block = value_block.reshape(3 * width_rows, head_count, HD)
        key_mask = jnp.concatenate([jnp.broadcast_to(flag, (width_rows,)) for flag in flags], 0)
        query_tile = queries[tile_index * tile_size : (tile_index + 1) * tile_size].reshape(
            tile_size, head_count, HD
        )
        grad_tile = attn_grad[tile_index * tile_size : (tile_index + 1) * tile_size].reshape(
            tile_size, head_count, HD
        )
        scores = (
            jnp.einsum("qhd,khd->hqk", query_tile, key_block, preferred_element_type=jnp.float32)
            * inverse_root
        )
        scores = jnp.where(key_mask[None, None, :], scores, -jnp.inf)
        row_peak = jnp.max(scores, axis=2, keepdims=True)
        weights = jnp.exp(scores - row_peak)
        row_total = jnp.sum(weights, axis=2, keepdims=True)
        softmax_rows = weights / row_total
        softmax_grad = jnp.einsum(
            "qhd,khd->hqk", grad_tile, value_block, preferred_element_type=jnp.float32
        )
        row_inner = jnp.sum(softmax_rows * softmax_grad, axis=2, keepdims=True)
        score_grad = (softmax_rows * (softmax_grad - row_inner)).astype(jnp.bfloat16)
        softmax_low = softmax_rows.astype(jnp.bfloat16)
        grad_query = (
            jnp.einsum("hqk,khd->qhd", score_grad, key_block, preferred_element_type=jnp.float32)
            * inverse_root
        )
        query_grads.append(grad_query.reshape(tile_size, local_width).astype(jnp.bfloat16))
        kept = (0, 1, 2)
        key_part = (
            jnp.einsum("hqk,qhd->khd", score_grad, query_tile, preferred_element_type=jnp.float32)
            * inverse_root
        )
        key_part = key_part.reshape(len(kept) * width_rows, local_width)
        value_part = jnp.einsum(
            "hqk,qhd->khd", softmax_low, grad_tile, preferred_element_type=jnp.float32
        )
        value_part = value_part.reshape(len(kept) * width_rows, local_width)
        for position, slab_index in enumerate(kept):
            for neighbour in range(lower, upper + 1):
                offset = position * width_rows + (neighbour - lower) * tile_size
                key_sums[slab_index][neighbour] = (
                    key_sums[slab_index][neighbour] + key_part[offset : offset + tile_size]
                )
                value_sums[slab_index][neighbour] = (
                    value_sums[slab_index][neighbour] + value_part[offset : offset + tile_size]
                )
    own_keys = jnp.concatenate(key_sums[1], 0)
    own_values = jnp.concatenate(value_sums[1], 0)
    later_keys, later_values = (
        passed_along(jnp.concatenate(key_sums[0], 0).astype(jnp.bfloat16), "tm", -1).astype(
            jnp.float32
        ),
        passed_along(jnp.concatenate(value_sums[0], 0).astype(jnp.bfloat16), "tm", -1).astype(
            jnp.float32
        ),
    )
    earlier_keys, earlier_values = (
        passed_along(jnp.concatenate(key_sums[2], 0).astype(jnp.bfloat16), "tm", 1).astype(
            jnp.float32
        ),
        passed_along(jnp.concatenate(value_sums[2], 0).astype(jnp.bfloat16), "tm", 1).astype(
            jnp.float32
        ),
    )
    grad_keys = own_keys + later_keys + earlier_keys
    grad_values = own_values + later_values + earlier_values
    grad_queries = jnp.concatenate(query_grads, 0)
    return (grad_queries, grad_keys.astype(jnp.bfloat16), grad_values.astype(jnp.bfloat16))


def solution(mesh):
    placed = (P("tm", "head"), P("tm", "head"), P("tm", "head"), P("tm", "head"), P("head", "tm"))
    return jax.shard_map(
        local,
        mesh=mesh,
        in_specs=placed,
        out_specs=(P("tm", "head"), P("tm", "head"), P("tm", "head")),
        check_vma=False,
    )
```

profile of v0, /device:TPU:0, one launch (start us, length us, event | category | flops | bytes accessed | tf_op | source)
XLA Modules:
  0.0 249.1 jit_solution(441162464719006397)
XLA Ops:
  11.3 6.4 %collective-permute-start.2 = (bf16[768,384]{0,1:T(8,128)(2,1)S(1)}, bf16[768,384]{0,1:T(8,128)(2,1)}, u32[]{:S(2)}, u32[]{:S(2)}) collective-permute-start(bf16[768,384]{0,1:T(8,128)(2,1)S(1)} %copy.44), channel_id=1, source_target_pairs={{0,4},{4,8},{8,12},{12,16},{16,20},{20,24},{24,28},{1,5},{5,9},{9,... | collective-permute-start | bytes 1769480 | tf_op jit(solution)/shard_map/ppermute | solution.py:17
  20.2 5.4 %collective-permute-start = (bf16[768,384]{0,1:T(8,128)(2,1)S(1)}, bf16[768,384]{0,1:T(8,128)(2,1)}, u32[]{:S(2)}, u32[]{:S(2)}) collective-permute-start(bf16[768,384]{0,1:T(8,128)(2,1)S(1)} %copy.38), channel_id=1, source_target_pairs={{0,4},{4,8},{8,12},{12,16},{16,20},{20,24},{24,28},{1,5},{5,9},{9,... | collective-permute-start | bytes 1769480 | tf_op jit(solution)/shard_map/ppermute | solution.py:17
  26.3 5.9 %collective-permute-done.3 = bf16[768,384]{0,1:T(8,128)(2,1)S(1)} collective-permute-done((bf16[768,384]{0,1:T(8,128)(2,1)S(1)}, bf16[768,384]{0,1:T(8,128)(2,1)S(1)}, u32[]{:S(2)}, u32[]{:S(2)}) %collective-permute-start.3) | collective-permute-done | bytes 589856 | tf_op jit(solution)/shard_map/ppermute | solution.py:17
  32.2 24.7 %collective-permute-done.2 = bf16[768,384]{0,1:T(8,128)(2,1)} collective-permute-done((bf16[768,384]{0,1:T(8,128)(2,1)S(1)}, bf16[768,384]{0,1:T(8,128)(2,1)}, u32[]{:S(2)}, u32[]{:S(2)}) %collective-permute-start.2) | collective-permute-done | bytes 589856 | tf_op jit(solution)/shard_map/ppermute | solution.py:17
  56.9 2.5 pad_maximum_fusion.1
  60.2 11.8 %collective-permute-done = bf16[768,384]{0,1:T(8,128)(2,1)} collective-permute-done((bf16[768,384]{0,1:T(8,128)(2,1)S(1)}, bf16[768,384]{0,1:T(8,128)(2,1)}, u32[]{:S(2)}, u32[]{:S(2)}) %collective-permute-start) | collective-permute-done | bytes 589856 | tf_op jit(solution)/shard_map/ppermute | solution.py:17
  73.4 7.7 %fusion.52 = (f32[3,384]{1,0:T(4,128)S(1)}, f32[3,384,2304]{1,2,0:T(8,128)}) fusion(pred[2304]{0:T(1024)(128)(4,1)S(1)} %pad_add_fusion, bf16[2304,3,128]{0,2,1:T(8,128)(2,1)S(1)} %bitcast.78, bf16[384,3,128]{0,2,1:T(8,128)(2,1)S(1)} %bitcast.95), kind=kOutput, calls=%fused_computation.81 | convolution fusion | flops 690096384 | bytes 12688128 | tf_op jit(solution)/shard_map/sub | solution.py:68
  81.0 7.8 %fusion.53 = (f32[3,384]{1,0:T(4,128)S(1)}, f32[3,384,2304]{1,2,0:T(8,128)}) fusion(pred[2304]{0:T(1024)(128)(4,1)S(1)} %pad_add_fusion, bf16[2304,3,128]{0,2,1:T(8,128)(2,1)S(1)} %bitcast.79, bf16[384,3,128]{0,2,1:T(8,128)(2,1)S(1)} %bitcast.92), kind=kOutput, calls=%fused_computation.82 | convolution fusion | flops 690096384 | bytes 12688128 | tf_op jit(solution)/shard_map/sub | solution.py:68
  88.9 3.6 %all-gather.5.cloned.1.call-done = bf16[384,3072]{1,0:T(8,128)(2,1)} async-done(((bf16[384,384]{1,0:T(8,128)(2,1)}), bf16[384,3072]{1,0:T(8,128)(2,1)}) %all-gather.5.cloned.1.call-update) | async-done | bytes 2359312 | tf_op jit(solution)/shard_map/all_gather | solution.py:36
  92.5 39.1 %all-gather.3.cloned.1.call-done = bf16[768,3072]{1,0:T(8,128)(2,1)} async-done(((bf16[768,768]{1,0:T(8,128)(2,1)}), bf16[768,3072]{1,0:T(8,128)(2,1)}) %all-gather.3.cloned.1.call-update) | async-done | bytes 4718608 | tf_op jit(solution)/shard_map/all_gather | solution.py:32
  131.6 5.1 %convolution_convert_fusion = bf16[768,384]{0,1:T(8,128)(2,1)S(1)} fusion(bf16[768,3072]{1,0:T(8,128)(2,1)} %all-gather.3.cloned.1.call-done, bf16[384,3072]{1,0:T(8,128)(2,1)} %all-gather.5.cloned.1.call-done), kind=kOutput, calls=%fused_computation.36 | convolution fusion | flops 1812234240 | bytes 7667712 | tf_op jit(solution)/shard_map/td,hd->th/dot_general | solution.py:33
  136.8 5.8 %fusion.25 = f32[2304,3,128]{0,2,1:T(8,128)S(1)} fusion(bf16[384,3,128]{0,2,1:T(8,128)(2,1)S(1)} %bitcast.108, f32[3,384,2304]{1,2,0:T(8,128)} %get-tuple-element.20, f32[3,384]{1,0:T(4,128)S(1)} %get-tuple-element.19), kind=kOutput, calls=%fused_computation.33 | convolution fusion | flops 684785664 | bytes 14455296 | tf_op jit(solution)/shard_map/hqk,qhd->khd/dot_general | solution.py:88
  144.3 5.0 %multiply_reduce_fusion = (f32[3,384]{1,0:T(4,128)S(1)}, f32[3,384,2304]{1,2,0:T(8,128)}) fusion(f32[3,384,2304]{1,2,0:T(8,128)S(1)} %bitcast.85, f32[3,384]{1,0:T(4,128)S(1)} %get-tuple-element.19, bf16[384,3,128]{0,2,1:T(8,128)(2,1)S(1)} %bitcast.109, bf16[2304,3,128]{0,2,1:T(8,128)(2,1)S(1)} %bitcast.90), kind=kOutput, calls=%fused_computation.11 | convolution fusion | flops 687438720 | bytes 23307264 | tf_op jit(solution)/shard_map/qhd,khd->hqk/dot_general | solution.py:71
  149.4 8.3 %multiply_convert_fusion = bf16[3,384,2304]{1,2,0:T(8,128)(2,1)S(1)} fusion(f32[3,384,2304]{1,2,0:T(8,128)} %get-tuple-element.22, f32[3,384]{1,0:T(4,128)S(1)} %get-tuple-element.21, f32[3,384,2304]{1,2,0:T(8,128)} %get-tuple-element.20, f32[3,384]{1,0:T(4,128)S(1)} %get-tuple-element.19), kind=kLoop, calls=%fused_computation.10 | loop fusion | flops 10616832 | bytes 26551296 | tf_op jit(solution)/shard_map/convert_element_type | solution.py:75
  159.5 3.4 %fusion.21 = f32[2304,3,128]{0,2,1:T(8,128)} fusion(bf16[3,384,2304]{1,2,0:T(8,128)(2,1)S(1)} %multiply_convert_fusion, bf16[384,3,128]{0,2,1:T(8,128)(2,1)S(1)} %bitcast.96), kind=kOutput, calls=%fused_computation.31 | convolution fusion | flops 680361984 | bytes 9142272 | tf_op jit(solution)/shard_map/hqk,qhd->khd/dot_general | solution.py:84
  164.5 5.0 %multiply_reduce_fusion.1 = (f32[3,384]{1,0:T(4,128)S(1)}, f32[3,384,2304]{1,2,0:T(8,128)}) fusion(f32[3,384,2304]{1,2,0:T(8,128)S(1)} %bitcast.83, f32[3,384]{1,0:T(4,128)S(1)} %get-tuple-element.23, bf16[384,3,128]{0,2,1:T(8,128)(2,1)S(1)} %bitcast.107, bf16[2304,3,128]{0,2,1:T(8,128)(2,1)S(1)} %bitcast.91), kind=kOutput, calls=%fused_computation.14 | convolution fusion | flops 687438720 | bytes 23307264 | tf_op jit(solution)/shard_map/qhd,khd->hqk/dot_general | solution.py:71
  177.2 2.0 pad_maximum_fusion.5
  182.4 5.4 %collective-permute-start.7 = (bf16[768,384]{1,0:T(8,128)(2,1)}, bf16[768,384]{1,0:T(8,128)(2,1)}, u32[]{:S(2)}, u32[]{:S(2)}) collective-permute-start(bf16[768,384]{1,0:T(8,128)(2,1)} %pad_maximum_fusion.6), channel_id=1, source_target_pairs={{0,4},{4,8},{8,12},{12,16},{16,20},{20,24},{24,28},{1,5},{5,9},{9,... | collective-permute-start | bytes 1769480 | tf_op jit(solution)/shard_map/ppermute | solution.py:17
  187.7 7.9 %multiply_convert_fusion.1 = bf16[3,384,2304]{1,2,0:T(8,128)(2,1)S(1)} fusion(f32[3,384,2304]{1,2,0:T(8,128)} %get-tuple-element.26, f32[3,384]{1,0:T(4,128)S(1)} %get-tuple-element.25, f32[3,384,2304]{1,2,0:T(8,128)} %get-tuple-element.24, f32[3,384]{1,0:T(4,128)S(1)} %get-tuple-element.23), kind=kLoop, calls=%fused_computation.13 | loop fusion | flops 10616832 | bytes 26551296 | tf_op jit(solution)/shard_map/convert_element_type | solution.py:75
  213.5 5.4 %collective-permute-start.5 = (bf16[768,384]{1,0:T(8,128)(2,1)}, bf16[768,384]{1,0:T(8,128)(2,1)}, u32[]{:S(2)}, u32[]{:S(2)}) collective-permute-start(bf16[768,384]{1,0:T(8,128)(2,1)} %pad_maximum_fusion.4), channel_id=1, source_target_pairs={{0,4},{4,8},{8,12},{12,16},{16,20},{20,24},{24,28},{1,5},{5,9},{9,... | collective-permute-start | bytes 1769480 | tf_op jit(solution)/shard_map/ppermute | solution.py:17
  218.9 4.3 %fusion.28 = bf16[3,128,384]{2,1,0:T(8,128)(2,1)} fusion(bf16[2304,3,128]{0,2,1:T(8,128)(2,1)S(1)} %bitcast.81, bf16[3,384,2304]{1,2,0:T(8,128)(2,1)} %copy-done), kind=kOutput, calls=%fused_computation.39 | convolution fusion | flops 679772160 | bytes 7372800 | tf_op jit(solution)/shard_map/hqk,khd->qhd/dot_general | solution.py:78
  229.1 2.2 fusion.33
  231.4 8.7 %collective-permute-done.5 = bf16[768,384]{1,0:T(8,128)(2,1)} collective-permute-done((bf16[768,384]{1,0:T(8,128)(2,1)}, bf16[768,384]{1,0:T(8,128)(2,1)}, u32[]{:S(2)}, u32[]{:S(2)}) %collective-permute-start.5) | collective-permute-done | bytes 589856 | tf_op jit(solution)/shard_map/ppermute | solution.py:17
  240.0 2.2 fusion.31
  (72 shorter events, 49.2 us)
Async XLA Ops:
  7.2 18.5 %copy-start.5 = (bf16[768,384]{1,0:T(8,128)(2,1)S(1)}, bf16[768,384]{1,0:T(8,128)(2,1)}, u32[]{:S(2)}) copy-start(bf16[768,384]{1,0:T(8,128)(2,1)} %param.5) | copy-start | bytes 1769476
  7.2 85.3 %all-gather.5.cloned.1.call-start = ((), (), s32[]{:S(2)}) async-start(), calls=%async_computation.1 | async-start | bytes 2654208 | tf_op jit(solution)/shard_map/all_gather | solution.py:36
  7.9 123.7 %all-gather.3.cloned.1.call-start = ((), (), s32[]{:S(2)}) async-start(), calls=%async_computation | async-start | bytes 5898240 | tf_op jit(solution)/shard_map/all_gather | solution.py:32
  10.0 22.2 %collective-permute-start.3 = (bf16[768,384]{0,1:T(8,128)(2,1)S(1)}, bf16[768,384]{0,1:T(8,128)(2,1)S(1)}, u32[]{:S(2)}, u32[]{:S(2)}) collective-permute-start(bf16[768,384]{0,1:T(8,128)(2,1)S(1)} %copy.44), channel_id=1, source_target_pairs={{4,0},{8,4},{12,8},{16,12},{20,16},{24,20},{28,24},{5,1},{9,5},{13... | collective-permute-start | bytes 1769480 | tf_op jit(solution)/shard_map/ppermute | solution.py:17
  11.3 45.6 %collective-permute-start.2 = (bf16[768,384]{0,1:T(8,128)(2,1)S(1)}, bf16[768,384]{0,1:T(8,128)(2,1)}, u32[]{:S(2)}, u32[]{:S(2)}) collective-permute-start(bf16[768,384]{0,1:T(8,128)(2,1)S(1)} %copy.44), channel_id=1, source_target_pairs={{0,4},{4,8},{8,12},{12,16},{16,20},{20,24},{24,28},{1,5},{5,9},{9,... | collective-permute-start | bytes 1769480 | tf_op jit(solution)/shard_map/ppermute | solution.py:17
  18.9 40.4 %collective-permute-start.1 = (bf16[768,384]{0,1:T(8,128)(2,1)S(1)}, bf16[768,384]{0,1:T(8,128)(2,1)S(1)}, u32[]{:S(2)}, u32[]{:S(2)}) collective-permute-start(bf16[768,384]{0,1:T(8,128)(2,1)S(1)} %copy.38), channel_id=1, source_target_pairs={{4,0},{8,4},{12,8},{16,12},{20,16},{24,20},{28,24},{5,1},{9,5},{13... | collective-permute-start | bytes 1769480 | tf_op jit(solution)/shard_map/ppermute | solution.py:17
  20.2 51.8 %collective-permute-start = (bf16[768,384]{0,1:T(8,128)(2,1)S(1)}, bf16[768,384]{0,1:T(8,128)(2,1)}, u32[]{:S(2)}, u32[]{:S(2)}) collective-permute-start(bf16[768,384]{0,1:T(8,128)(2,1)S(1)} %copy.38), channel_id=1, source_target_pairs={{0,4},{4,8},{8,12},{12,16},{16,20},{20,24},{24,28},{1,5},{5,9},{9,... | collective-permute-start | bytes 1769480 | tf_op jit(solution)/shard_map/ppermute | solution.py:17
  59.4 0.8 copy-start.4
  136.7 5.9 %slice-start.3 = ((s8[10616832]{0:T(1024)(128)(4,1)}), s8[4194304]{0:T(1024)(128)(4,1)S(1)}, s32[]{:S(2)}) async-start(s8[10616832]{0:T(1024)(128)(4,1)} %bitcast.84), calls=%async_computation.5 | async-start | bytes 8388608
  136.8 6.4 %slice-start.4 = ((s8[10616832]{0:T(1024)(128)(4,1)}), s8[4194304]{0:T(1024)(128)(4,1)S(1)}, s32[]{:S(2)}) async-start(s8[10616832]{0:T(1024)(128)(4,1)} %bitcast.84), calls=%async_computation.6 | async-start | bytes 8388608
  136.8 7.1 %slice-start.5 = ((s8[10616832]{0:T(1024)(128)(4,1)}), s8[2228224]{0:T(1024)(128)(4,1)S(1)}, s32[]{:S(2)}) async-start(s8[10616832]{0:T(1024)(128)(4,1)} %bitcast.84), calls=%async_computation.7 | async-start | bytes 4456448
  136.8 7.5 %copy-start.3 = (bf16[2304,384]{0,1:T(8,128)(2,1)S(1)}, bf16[2304,384]{0,1:T(8,128)(2,1)}, u32[]{:S(2)}) copy-start(bf16[2304,384]{0,1:T(8,128)(2,1)} %pad_maximum_fusion.1) | copy-start | bytes 5308420
  149.4 13.5 %slice-start = ((s8[10616832]{0:T(1024)(128)(4,1)}), s8[4194304]{0:T(1024)(128)(4,1)S(1)}, s32[]{:S(2)}) async-start(s8[10616832]{0:T(1024)(128)(4,1)} %bitcast.82), calls=%async_computation.2 | async-start | bytes 8388608
  149.4 13.5 %slice-start.1 = ((s8[10616832]{0:T(1024)(128)(4,1)}), s8[4194304]{0:T(1024)(128)(4,1)S(1)}, s32[]{:S(2)}) async-start(s8[10616832]{0:T(1024)(128)(4,1)} %bitcast.82), calls=%async_computation.3 | async-start | bytes 8388608
  157.7 5.2 %slice-start.2 = ((s8[10616832]{0:T(1024)(128)(4,1)}), s8[2228224]{0:T(1024)(128)(4,1)S(1)}, s32[]{:S(2)}) async-start(s8[10616832]{0:T(1024)(128)(4,1)} %bitcast.82), calls=%async_computation.4 | async-start | bytes 4456448
  179.2 49.9 %collective-permute-start.6 = (bf16[768,384]{1,0:T(8,128)(2,1)}, bf16[768,384]{1,0:T(8,128)(2,1)}, u32[]{:S(2)}, u32[]{:S(2)}) collective-permute-start(bf16[768,384]{1,0:T(8,128)(2,1)} %pad_maximum_fusion.5), channel_id=1, source_target_pairs={{4,0},{8,4},{12,8},{16,12},{20,16},{24,20},{28,24},{5,1},{9,5},{13... | collective-permute-start | bytes 1769480 | tf_op jit(solution)/shard_map/ppermute | solution.py:17
  182.4 46.7 %collective-permute-start.7 = (bf16[768,384]{1,0:T(8,128)(2,1)}, bf16[768,384]{1,0:T(8,128)(2,1)}, u32[]{:S(2)}, u32[]{:S(2)}) collective-permute-start(bf16[768,384]{1,0:T(8,128)(2,1)} %pad_maximum_fusion.6), channel_id=1, source_target_pairs={{0,4},{4,8},{8,12},{12,16},{16,20},{20,24},{24,28},{1,5},{5,9},{9,... | collective-permute-start | bytes 1769480 | tf_op jit(solution)/shard_map/ppermute | solution.py:17
  195.7 2.7 %copy-start = (bf16[3,384,2304]{1,2,0:T(8,128)(2,1)}, bf16[3,384,2304]{1,2,0:T(8,128)(2,1)S(1)}, u32[]{:S(2)}) copy-start(bf16[3,384,2304]{1,2,0:T(8,128)(2,1)S(1)} %multiply_convert_fusion.1) | copy-start | bytes 15925252
  195.7 3.9 %copy-start.1 = (f32[2304,3,128]{0,2,1:T(8,128)S(1)}, f32[2304,3,128]{0,2,1:T(8,128)}, u32[]{:S(2)}) copy-start(f32[2304,3,128]{0,2,1:T(8,128)} %fusion.21) | copy-start | bytes 10616836
  210.3 21.0 %collective-permute-start.4 = (bf16[768,384]{1,0:T(8,128)(2,1)}, bf16[768,384]{1,0:T(8,128)(2,1)}, u32[]{:S(2)}, u32[]{:S(2)}) collective-permute-start(bf16[768,384]{1,0:T(8,128)(2,1)} %pad_maximum_fusion.3), channel_id=1, source_target_pairs={{4,0},{8,4},{12,8},{16,12},{20,16},{24,20},{28,24},{5,1},{9,5},{13... | collective-permute-start | bytes 1769480 | tf_op jit(solution)/shard_map/ppermute | solution.py:17
  213.5 26.5 %collective-permute-start.5 = (bf16[768,384]{1,0:T(8,128)(2,1)}, bf16[768,384]{1,0:T(8,128)(2,1)}, u32[]{:S(2)}, u32[]{:S(2)}) collective-permute-start(bf16[768,384]{1,0:T(8,128)(2,1)} %pad_maximum_fusion.4), channel_id=1, source_target_pairs={{0,4},{4,8},{8,12},{12,16},{16,20},{20,24},{24,28},{1,5},{5,9},{9,... | collective-permute-start | bytes 1769480 | tf_op jit(solution)/shard_map/ppermute | solution.py:17
  223.2 3.6 %copy-start.2 = (f32[384,3,128]{0,2,1:T(8,128)S(1)}, f32[384,3,128]{0,2,1:T(8,128)}, u32[]{:S(2)}) copy-start(f32[384,3,128]{0,2,1:T(8,128)} %get-tuple-element.13) | copy-start | bytes 1769476
Sparse Core Ops, SparseCore 0:
  10.0 82.4 all-gather.4
  94.1 37.4 all-gather.2
where the time goes:
time: 250 us; the launch traced here: 249 us
  waiting for transfers between devices  95.2 us (38%)
  matrix products  49.2 us (20%)
  other arithmetic  36.7 us (15%)
  starting transfers between devices  27.8 us (11%)
  local copies, waits for them, and re-layouts  25.9 us (10%)
  between operations  14.3 us (6%)
    ppermute x8, waiting for transfers between devices, passed_along(): return lax.ppermute(block, axis, route)  51.1 us
    all_gather x1, waiting for transfers between devices, local(): full_grad = lax.all_gather(grad_out, 'head', axis=1, tiled=True)  39.1 us
    ppermute x8, starting transfers between devices, passed_along(): return lax.ppermute(block, axis, route)  27.7 us
    convert_element_type x2, other arithmetic, local(): (softmax_rows * (softmax_grad - row_inner)).astype(jnp.bfloat16)  16.2 us
    sub x2, matrix products, local(): weights = jnp.exp(scores - row_peak)  15.5 us
    dot_general x2, matrix products, local(): jnp.einsum('qhd,khd->hqk', grad_tile, value_block, preferred_element_type...  9.98 us
    add x6, local copies, waits for them, and re-layouts, local(): key_sums[slab_index][neighbour] + key_part[offset:offset + tile_size]  7.88 us
    unnamed x28, local copies, waits for them, and re-layouts  7.88 us
  transfers between devices with their start and end apart: 10, of which 6 were waited for; matrix products, arithmetic and copies ran while one was open for 24% of the time, Pallas kernels for 0%

commit v1 on v0

--- a/solution.py
+++ b/solution.py
@@ -29,7 +29,26 @@
     inverse_root = 1.0 / math.sqrt(HD)
     video_place = lax.axis_index("tm") % VT
     flags = (video_place > 0, video_place >= 0, video_place < VT - 1)
-    full_grad = lax.all_gather(grad_out, "head", axis=1, tiled=True)
+    work_now, raw_out, piece_now = (
+        lax.axis_size("head"),
+        lax.axis_index("head"),
+        grad_out.shape[1],
+    )
+    mixed_arr, outcome_arr = (grad_out, 1)
+    while outcome_arr < work_now:
+        mixed_arr = jnp.concatenate(
+            [
+                mixed_arr,
+                lax.ppermute(
+                    mixed_arr,
+                    axis_name="head",
+                    perm=tuple(((nth, (nth - outcome_arr) % work_now) for nth in range(work_now))),
+                ),
+            ],
+            axis=1,
+        )
+        outcome_arr = 2 * outcome_arr
+    full_grad = jnp.roll(mixed_arr, raw_out * piece_now, axis=1)
     attn_sum = jnp.einsum(
         "td,hd->th",
         full_grad,

time: 250 us -> 221 us (0.88)
  waiting for transfers between devices: 95.2 us -> 41.4 us
  local copies, waits for them, and re-layouts: 25.9 us -> 42.9 us
  matrix products: 49.2 us -> 53 us
  starting transfers between devices: 27.8 us -> 31.2 us
    all_gather x1 -> x0, waiting for transfers between devices: 39.1 us -> none  [local(): full_grad = lax.all_gather(grad_out, 'head', axis=1, tiled=True)]
    unnamed x28 -> x45, local copies, waits for them, and re-layouts: 7.88 us -> 18.9 us
    ppermute x8, waiting for transfers between devices: 51.1 us -> 41.4 us  [passed_along(): return lax.ppermute(block, axis, route)]
    all_gather x1, waiting for transfers between devices: 3.64 us -> 0.01 us  [local(): lax.all_gather(w_out, 'tm', axis=1, tiled=True)]
    ppermute x0 -> x2, starting transfers between devices: none -> 3.63 us  [local(): lax.ppermute(mixed_arr, axis_name='head', perm=tuple(((nth, (nth - outcom...]
    concatenate x0 -> x1, local copies, waits for them, and re-layouts: none -> 3.25 us  [local(): full_grad = jnp.roll(mixed_arr, raw_out * piece_now, axis=1)]
  transfers between devices with their start and end apart: 10 -> 11, of which waited for: 6 -> 3; matrix products, arithmetic and copies ran while one was open for 24% -> 37% of each run, Pallas kernels for 0% -> 0%
where the time goes in v1:
time: 221 us; the launch traced here: 219 us
  matrix products  53 us (24%)
  local copies, waits for them, and re-layouts  42.9 us (19%)
  waiting for transfers between devices  41.4 us (19%)
  other arithmetic  36.7 us (17%)
  starting transfers between devices  31.2 us (14%)
  between operations  14.3 us (6%)
    ppermute x8, waiting for transfers between devices, passed_along(): return lax.ppermute(block, axis, route)  41.4 us
    ppermute x8, starting transfers between devices, passed_along(): return lax.ppermute(block, axis, route)  27.5 us
    unnamed x45, local copies, waits for them, and re-layouts  18.9 us
    sub x2, matrix products, local(): weights = jnp.exp(scores - row_peak)  17.2 us
    convert_element_type x2, other arithmetic, local(): (softmax_rows * (softmax_grad - row_inner)).astype(jnp.bfloat16)  14.2 us
    dot_general x2, matrix products, local(): jnp.einsum('qhd,khd->hqk', grad_tile, value_block, preferred_element_type...  9.92 us
    dot_general x2, matrix products, local(): jnp.einsum('hqk,qhd->khd', softmax_low, grad_tile, preferred_element_type...  9.25 us
    add x6, local copies, waits for them, and re-layouts, local(): key_sums[slab_index][neighbour] + key_part[offset:offset + tile_size]  7.88 us
  transfers between devices with their start and end apart: 11, of which 3 were waited for; matrix products, arithmetic and copies ran while one was open for 37% of the time, Pallas kernels for 0%

profile of v1, /device:TPU:0, one launch (start us, length us, event | category | flops | bytes accessed | tf_op | source)
XLA Modules:
  0.0 219.5 jit_solution(13571025478446271425)
XLA Ops:
  7.2 2.5 %collective-permute-start.2 = (bf16[768,768]{1,0:T(8,128)(2,1)}, bf16[768,768]{1,0:T(8,128)(2,1)S(1)}, u32[]{:S(2)}, u32[]{:S(2)}) collective-permute-start(bf16[768,768]{1,0:T(8,128)(2,1)} %param.8), channel_id=1, source_target_pairs={{0,3},{1,0},{2,1},{3,2},{4,7},{5,4},{6,5},{7,6},{8,11},{9,8},{10,9... | collective-permute-start | bytes 3538952 | tf_op jit(solution)/shard_map/ppermute | solution.py:42
  12.3 5.4 %collective-permute-start.4 = (bf16[768,384]{0,1:T(8,128)(2,1)S(1)}, bf16[768,384]{0,1:T(8,128)(2,1)}, u32[]{:S(2)}, u32[]{:S(2)}) collective-permute-start(bf16[768,384]{0,1:T(8,128)(2,1)S(1)} %copy.44), channel_id=1, source_target_pairs={{0,4},{4,8},{8,12},{12,16},{16,20},{20,24},{24,28},{1,5},{5,9},{9,... | collective-permute-start | bytes 1769480 | tf_op jit(solution)/shard_map/ppermute | solution.py:17
  20.3 5.4 %collective-permute-start = (bf16[768,384]{0,1:T(8,128)(2,1)S(1)}, bf16[768,384]{0,1:T(8,128)(2,1)}, u32[]{:S(2)}, u32[]{:S(2)}) collective-permute-start(bf16[768,384]{0,1:T(8,128)(2,1)S(1)} %copy.38), channel_id=1, source_target_pairs={{0,4},{4,8},{8,12},{12,16},{16,20},{20,24},{24,28},{1,5},{5,9},{9,... | collective-permute-start | bytes 1769480 | tf_op jit(solution)/shard_map/ppermute | solution.py:17
  35.4 20.7 %collective-permute-done.4 = bf16[768,384]{0,1:T(8,128)(2,1)} collective-permute-done((bf16[768,384]{0,1:T(8,128)(2,1)S(1)}, bf16[768,384]{0,1:T(8,128)(2,1)}, u32[]{:S(2)}, u32[]{:S(2)}) %collective-permute-start.4) | collective-permute-done | bytes 589856 | tf_op jit(solution)/shard_map/ppermute | solution.py:17
  56.2 2.6 %pad_maximum_fusion.2 = bf16[2304,384]{0,1:T(8,128)(2,1)} fusion(bf16[768,384]{0,1:T(8,128)(2,1)} %collective-permute-done.5, bf16[768,384]{0,1:T(8,128)(2,1)S(1)} %copy.44, bf16[768,384]{0,1:T(8,128)(2,1)} %collective-permute-done.4), kind=kLoop, calls=%fused_computation.38 | loop fusion | flops 5308416 | bytes 3538944 | tf_op jit(solution)/shard_map/concatenate | solution.py:72
  58.7 12.6 %collective-permute-done = bf16[768,384]{0,1:T(8,128)(2,1)} collective-permute-done((bf16[768,384]{0,1:T(8,128)(2,1)S(1)}, bf16[768,384]{0,1:T(8,128)(2,1)}, u32[]{:S(2)}, u32[]{:S(2)}) %collective-permute-start) | collective-permute-done | bytes 589856 | tf_op jit(solution)/shard_map/ppermute | solution.py:17
  72.7 8.7 %fusion.58 = (f32[3,384]{1,0:T(4,128)S(1)}, f32[3,384,2304]{1,2,0:T(8,128)}) fusion(pred[2304]{0:T(1024)(128)(4,1)S(1)} %pad_add_fusion, bf16[2304,3,128]{0,2,1:T(8,128)(2,1)S(1)} %bitcast.77, bf16[384,3,128]{0,2,1:T(8,128)(2,1)} %bitcast.94), kind=kOutput, calls=%fused_computation.91 | convolution fusion | flops 690096384 | bytes 12688128 | tf_op jit(solution)/shard_map/sub | solution.py:87
  81.4 8.5 %fusion.59 = (f32[3,384]{1,0:T(4,128)S(1)}, f32[3,384,2304]{1,2,0:T(8,128)}) fusion(pred[2304]{0:T(1024)(128)(4,1)} %copy-done.11, bf16[2304,3,128]{0,2,1:T(8,128)(2,1)S(1)} %bitcast.78, bf16[384,3,128]{0,2,1:T(8,128)(2,1)S(1)} %bitcast.91), kind=kOutput, calls=%fused_computation.92 | convolution fusion | flops 690096384 | bytes 12688128 | tf_op jit(solution)/shard_map/sub | solution.py:87
  89.9 2.4 %constant_dynamic-update-slice_fusion.4 = bf16[768,6144]{1,0:T(8,128)(2,1)} fusion(bf16[768,6144]{1,0:T(8,128)(2,1)} %constant_dynamic-update-slice_fusion.5, bf16[768,768]{1,0:T(8,128)(2,1)} %copy-done.3), kind=kLoop, calls=%fused_computation.81 | loop fusion | bytes 2359296
  92.3 3.4 %constant_dynamic-update-slice_fusion.3 = bf16[768,6144]{1,0:T(8,128)(2,1)} fusion(bf16[768,6144]{1,0:T(8,128)(2,1)} %constant_dynamic-update-slice_fusion.4, bf16[768,1536]{1,0:T(8,128)(2,1)} %collective-permute-done.3), kind=kLoop, calls=%fused_computation.80 | loop fusion | bytes 4718592
  98.1 3.2 %constant_dynamic-update-slice_fusion = bf16[768,6144]{1,0:T(8,128)(2,1)} fusion(bf16[768,6144]{1,0:T(8,128)(2,1)} %constant_dynamic-update-slice_fusion.1, bf16[768,1536]{1,0:T(8,128)(2,1)} %collective-permute-done.3), kind=kLoop, calls=%fused_computation.77 | loop fusion | bytes 4718592 | tf_op jit(solution)/shard_map/jit(_roll_dynamic)/concatenate | solution.py:51
  101.3 5.5 %fusion.30 = bf16[768,384]{0,1:T(8,128)(2,1)S(1)} fusion(bf16[384,3072]{1,0:T(8,128)(2,1)} %all-gather.2.cloned.1.call-done, bf16[768,6144]{1,0:T(8,128)(2,1)} %constant_dynamic-update-slice_fusion, s32[]{:T(128)S(6)} %select_n.36), kind=kOutput, calls=%fused_computation.39 | convolution fusion | flops 1812234240 | bytes 7667716 | tf_op jit(solution)/shard_map/td,hd->th/dot_general | solution.py:52
  107.1 7.6 %fusion.27 = f32[2304,3,128]{0,2,1:T(8,128)} fusion(bf16[384,3,128]{0,2,1:T(8,128)(2,1)S(1)} %bitcast.107, f32[3,384,2304]{1,2,0:T(8,128)} %get-tuple-element.20, f32[3,384]{1,0:T(4,128)S(1)} %get-tuple-element.19), kind=kOutput, calls=%fused_computation.35 | convolution fusion | flops 684785664 | bytes 14455296 | tf_op jit(solution)/shard_map/hqk,qhd->khd/dot_general | solution.py:107
  115.8 4.9 %multiply_reduce_fusion = (f32[3,384]{1,0:T(4,128)S(1)}, f32[3,384,2304]{1,2,0:T(8,128)}) fusion(f32[3,384,2304]{1,2,0:T(8,128)S(1)} %bitcast.84, f32[3,384]{1,0:T(4,128)S(1)} %get-tuple-element.19, bf16[384,3,128]{0,2,1:T(8,128)(2,1)S(1)} %bitcast.108, bf16[2304,3,128]{0,2,1:T(8,128)(2,1)S(1)} %bitcast.89), kind=kOutput, calls=%fused_computation.11 | convolution fusion | flops 687438720 | bytes 23307264 | tf_op jit(solution)/shard_map/qhd,khd->hqk/dot_general | solution.py:90
  120.7 6.3 %multiply_convert_fusion = bf16[3,384,2304]{1,2,0:T(8,128)(2,1)S(1)} fusion(f32[3,384,2304]{1,2,0:T(8,128)} %get-tuple-element.22, f32[3,384]{1,0:T(4,128)S(1)} %get-tuple-element.21, f32[3,384,2304]{1,2,0:T(8,128)S(1)} %bitcast.84, f32[3,384]{1,0:T(4,128)S(1)} %get-tuple-element.19), kind=kLoop, calls=%fused_computation.10 | loop fusion | flops 10616832 | bytes 26551296 | tf_op jit(solution)/shard_map/convert_element_type | solution.py:94
  128.9 3.4 %fusion.23 = f32[2304,3,128]{0,2,1:T(8,128)} fusion(bf16[3,384,2304]{1,2,0:T(8,128)(2,1)S(1)} %multiply_convert_fusion, bf16[384,3,128]{0,2,1:T(8,128)(2,1)S(1)} %bitcast.95), kind=kOutput, calls=%fused_computation.33 | convolution fusion | flops 680361984 | bytes 9142272 | tf_op jit(solution)/shard_map/hqk,qhd->khd/dot_general | solution.py:103
  133.9 5.0 %multiply_reduce_fusion.1 = (f32[3,384]{1,0:T(4,128)S(1)}, f32[3,384,2304]{1,2,0:T(8,128)}) fusion(f32[3,384,2304]{1,2,0:T(8,128)S(1)} %bitcast.82, f32[3,384]{1,0:T(4,128)S(1)} %get-tuple-element.23, bf16[384,3,128]{0,2,1:T(8,128)(2,1)S(1)} %bitcast.106, bf16[2304,3,128]{0,2,1:T(8,128)(2,1)S(1)} %bitcast.90), kind=kOutput, calls=%fused_computation.14 | convolution fusion | flops 687438720 | bytes 23307264 | tf_op jit(solution)/shard_map/qhd,khd->hqk/dot_general | solution.py:90
  151.8 5.9 %collective-permute-start.9 = (bf16[768,384]{1,0:T(8,128)(2,1)}, bf16[768,384]{1,0:T(8,128)(2,1)}, u32[]{:S(2)}, u32[]{:S(2)}) collective-permute-start(bf16[768,384]{1,0:T(8,128)(2,1)} %pad_maximum_fusion.7), channel_id=1, source_target_pairs={{0,4},{4,8},{8,12},{12,16},{16,20},{20,24},{24,28},{1,5},{5,9},{9,... | collective-permute-start | bytes 1769480 | tf_op jit(solution)/shard_map/ppermute | solution.py:17
  157.7 8.0 %multiply_convert_fusion.1 = bf16[3,384,2304]{1,2,0:T(8,128)(2,1)S(1)} fusion(f32[3,384,2304]{1,2,0:T(8,128)} %get-tuple-element.26, f32[3,384]{1,0:T(4,128)S(1)} %get-tuple-element.25, f32[3,384,2304]{1,2,0:T(8,128)} %get-tuple-element.24, f32[3,384]{1,0:T(4,128)S(1)} %get-tuple-element.23), kind=kLoop, calls=%fused_computation.13 | loop fusion | flops 10616832 | bytes 26551296 | tf_op jit(solution)/shard_map/convert_element_type | solution.py:94
  183.5 5.7 %collective-permute-start.7 = (bf16[768,384]{1,0:T(8,128)(2,1)}, bf16[768,384]{1,0:T(8,128)(2,1)}, u32[]{:S(2)}, u32[]{:S(2)}) collective-permute-start(bf16[768,384]{1,0:T(8,128)(2,1)} %pad_maximum_fusion.5), channel_id=1, source_target_pairs={{0,4},{4,8},{8,12},{12,16},{16,20},{20,24},{24,28},{1,5},{5,9},{9,... | collective-permute-start | bytes 1769480 | tf_op jit(solution)/shard_map/ppermute | solution.py:17
  189.2 4.3 %fusion.33 = bf16[3,128,384]{2,1,0:T(8,128)(2,1)} fusion(bf16[2304,3,128]{0,2,1:T(8,128)(2,1)S(1)} %bitcast.80, bf16[3,384,2304]{1,2,0:T(8,128)(2,1)} %copy-done), kind=kOutput, calls=%fused_computation.42 | convolution fusion | flops 679772160 | bytes 7372800 | tf_op jit(solution)/shard_map/hqk,khd->qhd/dot_general | solution.py:97
  200.1 2.2 %fusion.38 = bf16[768,384]{1,0:T(8,128)(2,1)} fusion(f32[384,384]{1,0:T(8,128)S(1)} %copy.73, f32[384,384]{1,0:T(8,128)S(1)} %copy.72, bf16[768,384]{1,0:T(8,128)(2,1)} %collective-permute-done.9, bf16[768,384]{1,0:T(8,128)(2,1)} %collective-permute-done.8), kind=kLoop, calls=%fused_computation.49 | loop fusion | flops 1769472 | bytes 2949120 | tf_op jit(solution)/shard_map/convert_element_type | solution.py:141
  202.4 8.0 %collective-permute-done.7 = bf16[768,384]{1,0:T(8,128)(2,1)} collective-permute-done((bf16[768,384]{1,0:T(8,128)(2,1)}, bf16[768,384]{1,0:T(8,128)(2,1)}, u32[]{:S(2)}, u32[]{:S(2)}) %collective-permute-start.7) | collective-permute-done | bytes 589856 | tf_op jit(solution)/shard_map/ppermute | solution.py:17
  210.4 2.2 %fusion.36 = bf16[768,384]{1,0:T(8,128)(2,1)} fusion(f32[384,384]{1,0:T(8,128)S(1)} %copy.65, f32[384,384]{1,0:T(8,128)S(1)} %copy.64, bf16[768,384]{1,0:T(8,128)(2,1)} %collective-permute-done.7, bf16[768,384]{1,0:T(8,128)(2,1)} %collective-permute-done.6), kind=kLoop, calls=%fused_computation.46 | loop fusion | flops 1769472 | bytes 2949120 | tf_op jit(solution)/shard_map/convert_element_type | solution.py:141
  (92 shorter events, 60.7 us)
Async XLA Ops:
  7.2 20.4 %copy-start.2 = (bf16[768,768]{1,0:T(8,128)(2,1)S(1)}, bf16[768,768]{1,0:T(8,128)(2,1)}, u32[]{:S(2)}) copy-start(bf16[768,768]{1,0:T(8,128)(2,1)} %param.8) | copy-start | bytes 3538948
  7.2 94.1 %all-gather.2.cloned.1.call-start = ((), (), s32[]{:S(2)}) async-start(), calls=%async_computation | async-start | bytes 2654208 | tf_op jit(solution)/shard_map/all_gather | solution.py:55
  7.2 20.4 %collective-permute-start.2 = (bf16[768,768]{1,0:T(8,128)(2,1)}, bf16[768,768]{1,0:T(8,128)(2,1)S(1)}, u32[]{:S(2)}, u32[]{:S(2)}) collective-permute-start(bf16[768,768]{1,0:T(8,128)(2,1)} %param.8), channel_id=1, source_target_pairs={{0,3},{1,0},{2,1},{3,2},{4,7},{5,4},{6,5},{7,6},{8,11},{9,8},{10,9... | collective-permute-start | bytes 3538952 | tf_op jit(solution)/shard_map/ppermute | solution.py:42
  11.0 24.4 %collective-permute-start.5 = (bf16[768,384]{0,1:T(8,128)(2,1)S(1)}, bf16[768,384]{0,1:T(8,128)(2,1)}, u32[]{:S(2)}, u32[]{:S(2)}) collective-permute-start(bf16[768,384]{0,1:T(8,128)(2,1)S(1)} %copy.44), channel_id=1, source_target_pairs={{4,0},{8,4},{12,8},{16,12},{20,16},{24,20},{28,24},{5,1},{9,5},{13... | collective-permute-start | bytes 1769480 | tf_op jit(solution)/shard_map/ppermute | solution.py:17
  12.3 43.9 %collective-permute-start.4 = (bf16[768,384]{0,1:T(8,128)(2,1)S(1)}, bf16[768,384]{0,1:T(8,128)(2,1)}, u32[]{:S(2)}, u32[]{:S(2)}) collective-permute-start(bf16[768,384]{0,1:T(8,128)(2,1)S(1)} %copy.44), channel_id=1, source_target_pairs={{0,4},{4,8},{8,12},{12,16},{16,20},{20,24},{24,28},{1,5},{5,9},{9,... | collective-permute-start | bytes 1769480 | tf_op jit(solution)/shard_map/ppermute | solution.py:17
  19.0 39.8 %collective-permute-start.1 = (bf16[768,384]{0,1:T(8,128)(2,1)S(1)}, bf16[768,384]{0,1:T(8,128)(2,1)}, u32[]{:S(2)}, u32[]{:S(2)}) collective-permute-start(bf16[768,384]{0,1:T(8,128)(2,1)S(1)} %copy.38), channel_id=1, source_target_pairs={{4,0},{8,4},{12,8},{16,12},{20,16},{24,20},{28,24},{5,1},{9,5},{13... | collective-permute-start | bytes 1769480 | tf_op jit(solution)/shard_map/ppermute | solution.py:17
  20.3 51.0 %collective-permute-start = (bf16[768,384]{0,1:T(8,128)(2,1)S(1)}, bf16[768,384]{0,1:T(8,128)(2,1)}, u32[]{:S(2)}, u32[]{:S(2)}) collective-permute-start(bf16[768,384]{0,1:T(8,128)(2,1)S(1)} %copy.38), channel_id=1, source_target_pairs={{0,4},{4,8},{8,12},{12,16},{16,20},{20,24},{24,28},{1,5},{5,9},{9,... | collective-permute-start | bytes 1769480 | tf_op jit(solution)/shard_map/ppermute | solution.py:17
  27.6 7.8 %copy-start.3 = (bf16[768,768]{1,0:T(8,128)(2,1)}, bf16[768,768]{1,0:T(8,128)(2,1)S(1)}, u32[]{:S(2)}) copy-start(bf16[768,768]{1,0:T(8,128)(2,1)S(1)} %collective-permute-done.2) | copy-start | bytes 3538948
  29.4 63.0 %collective-permute-start.3 = (bf16[768,1536]{1,0:T(8,128)(2,1)}, bf16[768,1536]{1,0:T(8,128)(2,1)}, u32[]{:S(2)}, u32[]{:S(2)}) collective-permute-start(bf16[768,1536]{1,0:T(8,128)(2,1)} %pad_maximum_fusion), channel_id=1, source_target_pairs={{0,2},{1,3},{2,0},{3,1},{4,6},{5,7},{6,4},{7,5},{8,10},{9,11},{10,... | collective-permute-start | bytes 7077896 | tf_op jit(solution)/shard_map/ppermute | solution.py:42
  30.6 42.1 %copy-start.11 = (pred[2304]{0:T(1024)(128)(4,1)}, pred[2304]{0:T(1024)(128)(4,1)S(1)}, u32[]{:S(2)}) copy-start(pred[2304]{0:T(1024)(128)(4,1)S(1)} %pad_add_fusion) | copy-start | bytes 6916
  72.7 8.7 %copy-start.9 = (bf16[384,384]{0,1:T(8,128)(2,1)S(1)}, bf16[384,384]{0,1:T(8,128)(2,1)}, u32[]{:S(2)}) copy-start(bf16[384,384]{0,1:T(8,128)(2,1)} %copy.94) | copy-start | bytes 884740
  92.3 4.6 %copy-start.4 = (bf16[768,768]{1,0:T(8,128)(2,1)S(1)}, bf16[768,768]{1,0:T(8,128)(2,1)}, u32[]{:S(2)}) copy-start(bf16[768,768]{1,0:T(8,128)(2,1)} %copy-done.3) | copy-start | bytes 3538948
  106.8 7.9 %slice-start.3 = ((s8[10616832]{0:T(1024)(128)(4,1)}), s8[4194304]{0:T(1024)(128)(4,1)S(1)}, s32[]{:S(2)}) async-start(s8[10616832]{0:T(1024)(128)(4,1)} %bitcast.83), calls=%async_computation.4 | async-start | bytes 8388608
  107.1 7.7 %slice-start.4 = ((s8[10616832]{0:T(1024)(128)(4,1)}), s8[4194304]{0:T(1024)(128)(4,1)S(1)}, s32[]{:S(2)}) async-start(s8[10616832]{0:T(1024)(128)(4,1)} %bitcast.83), calls=%async_computation.5 | async-start | bytes 8388608
  107.1 7.6 %slice-start.5 = ((s8[10616832]{0:T(1024)(128)(4,1)}), s8[2228224]{0:T(1024)(128)(4,1)S(1)}, s32[]{:S(2)}) async-start(s8[10616832]{0:T(1024)(128)(4,1)} %bitcast.83), calls=%async_computation.6 | async-start | bytes 4456448
  107.1 8.6 %copy-start.7 = (bf16[2304,384]{0,1:T(8,128)(2,1)S(1)}, bf16[2304,384]{0,1:T(8,128)(2,1)}, u32[]{:S(2)}) copy-start(bf16[2304,384]{0,1:T(8,128)(2,1)} %pad_maximum_fusion.2) | copy-start | bytes 5308420
  120.7 11.5 %slice-start = ((s8[10616832]{0:T(1024)(128)(4,1)}), s8[4194304]{0:T(1024)(128)(4,1)S(1)}, s32[]{:S(2)}) async-start(s8[10616832]{0:T(1024)(128)(4,1)} %bitcast.81), calls=%async_computation.1 | async-start | bytes 8388608
  120.7 11.5 %slice-start.1 = ((s8[10616832]{0:T(1024)(128)(4,1)}), s8[4194304]{0:T(1024)(128)(4,1)S(1)}, s32[]{:S(2)}) async-start(s8[10616832]{0:T(1024)(128)(4,1)} %bitcast.81), calls=%async_computation.2 | async-start | bytes 8388608
  127.0 5.2 %slice-start.2 = ((s8[10616832]{0:T(1024)(128)(4,1)}), s8[2228224]{0:T(1024)(128)(4,1)S(1)}, s32[]{:S(2)}) async-start(s8[10616832]{0:T(1024)(128)(4,1)} %bitcast.81), calls=%async_computation.3 | async-start | bytes 4456448
  133.9 5.0 %copy-start.5 = (f32[2304,3,128]{0,2,1:T(8,128)S(1)}, f32[2304,3,128]{0,2,1:T(8,128)}, u32[]{:S(2)}) copy-start(f32[2304,3,128]{0,2,1:T(8,128)} %fusion.27) | copy-start | bytes 10616836
  148.5 51.6 %collective-permute-start.8 = (bf16[768,384]{1,0:T(8,128)(2,1)}, bf16[768,384]{1,0:T(8,128)(2,1)}, u32[]{:S(2)}, u32[]{:S(2)}) collective-permute-start(bf16[768,384]{1,0:T(8,128)(2,1)} %pad_maximum_fusion.6), channel_id=1, source_target_pairs={{4,0},{8,4},{12,8},{16,12},{20,16},{24,20},{28,24},{5,1},{9,5},{13... | collective-permute-start | bytes 1769480 | tf_op jit(solution)/shard_map/ppermute | solution.py:17
  151.8 48.4 %collective-permute-start.9 = (bf16[768,384]{1,0:T(8,128)(2,1)}, bf16[768,384]{1,0:T(8,128)(2,1)}, u32[]{:S(2)}, u32[]{:S(2)}) collective-permute-start(bf16[768,384]{1,0:T(8,128)(2,1)} %pad_maximum_fusion.7), channel_id=1, source_target_pairs={{0,4},{4,8},{8,12},{12,16},{16,20},{20,24},{24,28},{1,5},{5,9},{9,... | collective-permute-start | bytes 1769480 | tf_op jit(solution)/shard_map/ppermute | solution.py:17
  180.3 22.1 %collective-permute-start.6 = (bf16[768,384]{1,0:T(8,128)(2,1)}, bf16[768,384]{1,0:T(8,128)(2,1)}, u32[]{:S(2)}, u32[]{:S(2)}) collective-permute-start(bf16[768,384]{1,0:T(8,128)(2,1)} %pad_maximum_fusion.4), channel_id=1, source_target_pairs={{4,0},{8,4},{12,8},{16,12},{20,16},{24,20},{28,24},{5,1},{9,5},{13... | collective-permute-start | bytes 1769480 | tf_op jit(solution)/shard_map/ppermute | solution.py:17
  183.5 26.9 %collective-permute-start.7 = (bf16[768,384]{1,0:T(8,128)(2,1)}, bf16[768,384]{1,0:T(8,128)(2,1)}, u32[]{:S(2)}, u32[]{:S(2)}) collective-permute-start(bf16[768,384]{1,0:T(8,128)(2,1)} %pad_maximum_fusion.5), channel_id=1, source_target_pairs={{0,4},{4,8},{8,12},{12,16},{16,20},{20,24},{24,28},{1,5},{5,9},{9,... | collective-permute-start | bytes 1769480 | tf_op jit(solution)/shard_map/ppermute | solution.py:17
  (5 other events, 14.4 us)
Sparse Core Ops, SparseCore 0:
  10.0 81.7 all-gather.1
